TPU v7x, 32 devices: a whole 2x2x4 slice. The times are simulated.
32 devices in a mesh: groups: 2 (over y), rows: 4 (over z), cols: 2 (over x), chan: 2 (over core).
Axes of the slice: x: 2, y: 2, z: 4, core: 2. Of those that a mesh axis runs over, the one named last changes fastest.
Arguments:
- tokens: bfloat16 [128, 128, 192], P(('groups', 'rows'), 'cols', 'chan'), parts along dimension 0, may hold values from -6 to 6
- tile_mask: int32 [2, 2], P('groups'), parts along dimension 0, may hold values 0 or 1
- ln_gain: float32 [192], replicated, may hold values from 0.1 to 1.9
- w_in_x: bfloat16 [192, 384], P(None, 'chan'), may hold values from -0.4375 to 0.4375
- w_in_z: bfloat16 [192, 384], P(None, 'chan'), may hold values from -0.4375 to 0.4375
- conv_w: float32 [3, 3, 384], P(None, None, 'chan'), may hold values from -2 to 2
- conv_b: float32 [384], P('chan'), may hold values from -0.5 to 0.5
- gate_scale: float32 [4, 384], P(None, 'chan'), may hold values from 0.5 to 2
- gate_bias: float32 [4, 384], P(None, 'chan'), may hold values from -8.5 to -1, as said below
- norm_gain: float32 [384], P('chan'), may hold values from 0.1 to 1.9
- w_out: bfloat16 [384, 192], P('chan'), may hold values from -0.3125 to 0.3125
Outputs:
- mixed: bfloat16 [128, 128, 192], P(('groups', 'rows'), 'cols', 'chan'), parts along dimension 0
There are 2 independent parts, one for each index of `groups`. A program takes and returns all parts, laid end to end along the dimension named above; an argument that names none is the same for every part. Nothing has to cross between parts.
Inputs may be any that keep to these rules, and one draw needn't show every extreme that they name: `gate_bias`: for each direction, some channels take values near minus the log of the scan's length and others near minus the log of 30 to 50.
All inputs are finite; a program needn't handle non-finite values.
Results may differ from a plain program's by a relative error of at most 0.009.
Values may be sent and summed in bfloat16 or wider, within the bound.
A program may use at most 64 MiB of HBM per device.

v0:
```python
import functools

import jax
import jax.numpy as jnp
from jax import lax
from jax.experimental import pallas as pl
from jax.experimental.pallas import tpu as pltpu
from jax.sharding import PartitionSpec as P

TILE = 64
LANES = 128
F32 = jnp.float32
BF16 = jnp.bfloat16
MESH = pl.DeviceIdType.MESH


def ln_pair(own, other, gain_own, gain_other):
    count = own.shape[-1] + other.shape[-1]
    mean = jnp.sum(own + other, -1, keepdims=True) / count
    own = own - mean
    other = other - mean
    var = jnp.sum(own * own + other * other, -1, keepdims=True) / count
    rstd = lax.rsqrt(var + 1e-05)
    return (own * rstd * gain_own).astype(BF16), (other * rstd * gain_other).astype(BF16)


def silu(x):
    half = 0.5 * x
    return half + half * jnp.tanh(half)


def kernel(
    n_rows, n_cols, pitch,
    *refs,
):
    held, out, staged = refs[:11], refs[11], refs[12:23]
    sem_in, sem_ready = refs[23:25]
    body(n_rows, n_cols, pitch, held, staged, sem_in, sem_ready, *staged, out, *refs[25:])


def body(
    n_rows, n_cols, pitch, held, staged, sem_in, sem_ready,
    tok, tile_mask, ln_gain, w_x, w_z, conv_w, conv_b, gate_scale, gate_bias, norm_gain, w_out,
    out,
    tok_other, cells, edge, halo, wx, wz, wo, par, gpar, normed, halo_u, upad, u,
    pv, kv, ph, kh, zs, sm, gated, vtot, packed, vsend, vrecv, hsend, hrecv, cv, ch, st, st_other, psend, precv, pown,
    sem_tok, sem_halo_s, sem_halo_r, sem_v_s, sem_v_r, sem_h_s, sem_h_r, sem_st, sem_p,
):
    r, c, k = (lax.axis_index(name) for name in ("rows", "cols", "chan"))
    o = 1 - k
    rows, cols, part = tok.shape
    width = w_x.shape[1]
    tiles = wx.shape[-1] // LANES

    def at(dr, dc, chan):
        return {"rows": r + dr, "cols": c + dc, "chan": chan}

    up, down, left, right = r > 0, r < n_rows - 1, c > 0, c < n_cols - 1
    base = 2 * cols
    corner = base + 2 * rows
    neighbours = (
        (up, -1, 0, tok.at[0], cols, cols),
        (down, 1, 0, tok.at[rows - 1], 0, cols),
        (left, 0, -1, edge.at[pl.ds(0, rows)], base + rows, rows),
        (right, 0, 1, edge.at[pl.ds(rows, rows)], base, rows),
        (up & left, -1, -1, tok.at[0, pl.ds(0, 16)], corner + 48, 16),
        (up & right, -1, 1, tok.at[0, pl.ds(cols - 16, 16)], corner + 32, 16),
        (down & left, 1, -1, tok.at[rows - 1, pl.ds(0, 16)], corner + 16, 16),
        (down & right, 1, 1, tok.at[rows - 1, pl.ds(cols - 16, 16)], corner, 16),
    )
    mirror = (1, 0, 3, 2, 7, 6, 5, 4)

    barrier = pltpu.get_barrier_semaphore()
    expected = jnp.int32(1)
    pl.semaphore_signal(barrier, inc=1, device_id=at(0, 0, o), device_id_type=MESH)
    for present, dr, dc, *_rest in neighbours:
        for chan in (k, o):

            @pl.when(present)
            def _():
                pl.semaphore_signal(barrier, inc=1, device_id=at(dr, dc, chan), device_id_type=MESH)

        expected = expected + 2 * present.astype(jnp.int32)

    loads = [pltpu.make_async_copy(held[n], staged[n], sem_in.at[n]) for n in range(len(held))]
    for load in loads:
        load.start()

    for n, (present, *_rest) in enumerate(neighbours):
        start, size = neighbours[mirror[n]][4], neighbours[n][5]

        @pl.when(jnp.logical_not(present))
        def _():
            halo[:, pl.ds(start, size), :] = jnp.zeros((2, size, part), BF16)

    loads[0].wait()
    cells[...] = jnp.zeros(cells.shape, F32)
    for i in range(rows):
        cells[pl.ds(32 * i, 16), 0:part] = tok[i, 0:16, :].astype(F32)
        cells[pl.ds(32 * i + 16, 16), 0:part] = tok[i, cols - 16 : cols, :].astype(F32)
    edge[pl.ds(0, rows), :] = cells[pl.ds(0, rows, stride=32), :][:, 0:part].astype(BF16)
    edge[pl.ds(rows, rows), :] = cells[pl.ds(31, rows, stride=32), :][:, 0:part].astype(BF16)

    pl.semaphore_wait(barrier, expected)

    axes = [(0, n_rows, r, "rows"), (1, n_cols, c, "cols")]

    def pass_on(far):
        for a, count, mine, name in axes:
            for d in range(2 if far < count else 0):
                step = -1 if d else 1
                subject, target = mine + step * (far - 1), mine - step

                @pl.when((subject >= 0) & (subject < count) & (target >= 0) & (target < count))
                def _():
                    pl.semaphore_signal(
                        sem_ready.at[a, d, far], inc=1, device_id={name: target}, device_id_type=MESH
                    )

    def hear(far):
        for a, count, mine, name in axes:
            for d in range(2 if far < count else 0):
                subject = mine + (-far if d else far)

                @pl.when((subject >= 0) & (subject < count))
                def _():
                    pl.semaphore_wait(sem_ready.at[a, d, far], 1)

    most = max(n_rows, n_cols)

    bands = 2
    band = rows // bands

    def tok_copy(g):
        place = pl.ds(g * band, band)
        return pltpu.make_async_remote_copy(
            tok.at[place], tok_other.at[place], sem_tok.at[0, g], sem_tok.at[1, g],
            device_id=at(0, 0, o), device_id_type=MESH,
        )

    for g in range(bands):
        tok_copy(g).start()

    def halo_copy(n, turn, chan):
        _, dr, dc, source, place, size = neighbours[n]
        return pltpu.make_async_remote_copy(
            source,
            halo.at[k, pl.ds(place, size)],
            sem_halo_s.at[n, turn],
            sem_halo_r.at[mirror[n], k],
            device_id=at(dr, dc, chan),
            device_id_type=MESH,
        )

    for n, (present, *_rest) in enumerate(neighbours):

        @pl.when(present)
        def _():
            for turn, chan in enumerate((k, o)):
                halo_copy(n, turn, chan).start()

    pass_on(2)

    for load in loads[1:]:
        load.wait()

    wx[...] = jnp.zeros(wx.shape, BF16)
    wz[...] = jnp.zeros(wz.shape, BF16)
    for slot, chan in enumerate((k, o)):
        place = pl.ds(pl.multiple_of(chan * part, 16), part)
        wx[slot, :, 0:width] = w_x[place, :]
        wz[slot, :, 0:width] = w_z[place, :]
    wo[...] = jnp.zeros(wo.shape, BF16)
    first, second = w_out[:, 0:part].astype(F32), w_out[:, part : 2 * part].astype(F32)
    wo[0:width, 0:part] = jnp.where(k == 0, first, second).astype(BF16)
    wo[0:width, LANES : LANES + part] = jnp.where(k == 0, second, first).astype(BF16)
    par[...] = jnp.zeros(par.shape, F32)
    for di in range(3):
        par[pl.ds(3 * di, 3), 0:width] = conv_w[di]
    par[9:10, 0:width] = conv_b[...]
    par[10:11, 0:width] = norm_gain[...]
    gpar[...] = jnp.zeros(gpar.shape, F32)
    scale, bias = 0.5 * gate_scale[...], 0.5 * gate_bias[...]
    for t in range(tiles):
        lo, hi = t * LANES, min(width, (t + 1) * LANES)
        gpar[t, 0:4, 0 : hi - lo] = scale[:, lo:hi]
        gpar[t, 4:8, 0 : hi - lo] = bias[:, lo:hi]
    gain = ln_gain[...]
    gain_own = jnp.where(k == 0, gain[:, 0:part], gain[:, part : 2 * part])
    gain_other = jnp.where(k == 0, gain[:, part : 2 * part], gain[:, 0:part])
    half_mask = 0.5 * tile_mask[r * rows // TILE, c * cols // TILE].astype(F32)


    def norm_row(i, carry):
        a, b = ln_pair(tok[i].astype(F32), tok_other[i].astype(F32), gain_own, gain_other)
        normed[0, i] = a
        normed[1, i] = b
        return carry

    for g in range(bands):
        tok_copy(g).wait_recv()
        lax.fori_loop(g * band, (g + 1) * band, norm_row, 0, unroll=True)
    step_rows = 4

    def product(q, weights):
        place = pl.ds(q * step_rows, step_rows)
        return jnp.dot(
            normed[0, place].reshape(step_rows * cols, part), weights[0], preferred_element_type=F32
        ) + jnp.dot(
            normed[1, place].reshape(step_rows * cols, part), weights[1], preferred_element_type=F32
        )

    def product_x(q, carry):
        value = product(q, wx).astype(BF16).astype(F32)
        for t in range(tiles):
            upad[t, pl.ds(q * step_rows + 1, step_rows), 8 : 8 + cols, :] = value[
                :, t * LANES : (t + 1) * LANES
            ].reshape(step_rows, cols, LANES)
        return carry

    lax.fori_loop(0, rows // step_rows, product_x, 0, unroll=True)

    for far in range(2, most):
        hear(far)
        pass_on(far + 1)

    for n, (present, *_rest) in enumerate(neighbours):
        place, size = neighbours[mirror[n]][4], neighbours[n][5]

        @pl.when(present)
        def _():
            for chan in (0, 1):
                landed = halo.at[chan, pl.ds(place, size)]
                pltpu.make_async_remote_copy(
                    landed, landed, sem_halo_s.at[n, 0], sem_halo_r.at[n, chan],
                    device_id=at(0, 0, o), device_id_type=MESH,
                ).wait_recv()

    a, b = ln_pair(halo[k].astype(F32), halo[o].astype(F32), gain_own, gain_other)
    ring = jnp.dot(a, wx[0], preferred_element_type=F32) + jnp.dot(b, wx[1], preferred_element_type=F32)
    halo_u[...] = ring.astype(BF16).astype(F32)
    for t in range(tiles):
        lanes = pl.ds(t * LANES, LANES)
        upad[t, 0, 8 : 8 + cols, :] = halo_u[0:cols, lanes]
        upad[t, rows + 1, 8 : 8 + cols, :] = halo_u[cols : 2 * cols, lanes]
        for i in range(rows):
            upad[t, 1 + i, 7:8, :] = halo_u[base + i : base + i + 1, lanes]
            upad[t, 1 + i, 8 + cols : 9 + cols, :] = halo_u[base + rows + i : base + rows + i + 1, lanes]
        upad[t, 0, 7:8, :] = halo_u[corner + 15 : corner + 16, lanes]
        upad[t, 0, 8 + cols : 9 + cols, :] = halo_u[corner + 16 : corner + 17, lanes]
        upad[t, rows + 1, 7:8, :] = halo_u[corner + 47 : corner + 48, lanes]
        upad[t, rows + 1, 8 + cols : 9 + cols, :] = halo_u[corner + 48 : corner + 49, lanes]

    def conv_row(i, carry):
        place = pl.ds(pl.multiple_of(i * pitch, 8), cols)
        for t in range(tiles):
            lanes = pl.ds(t * LANES, LANES)
            total = jnp.broadcast_to(par[9:10, lanes], (cols, LANES))
            for di in range(3):
                for dj in range(3):
                    tap = 3 * di + dj
                    total = total + par[tap : tap + 1, lanes] * upad[t, i + di, 7 + dj : 7 + dj + cols, :]
            u[t, place, :] = silu(total).astype(BF16).astype(F32)
        return carry

    lax.fori_loop(0, rows, conv_row, 0, unroll=2)

    span = 16
    per = cols // span

    def vertical(q, carry):
        t = q // per
        col = pl.multiple_of((q % per) * span, span)
        params = gpar[t]
        state = [[jnp.zeros((span, LANES), F32), jnp.ones((span, LANES), F32)] for _ in range(2)]
        for i in range(rows):
            for d in range(2):
                at_row = rows - 1 - i if d else i
                value = u[t, pl.ds(at_row * pitch + col, span), :]
                gate = half_mask + half_mask * jnp.tanh(params[2 + d : 3 + d] * value + params[6 + d : 7 + d])
                keep = 1.0 - gate
                state[d][0] = keep * state[d][0] + gate * value
                state[d][1] = keep * state[d][1]
                place = pl.ds(at_row * cols + col, span)
                pv[d, t, place, :] = state[d][0]
                kv[d, t, place, :] = state[d][1]
        for d in range(2):
            for j in range(2):
                vtot[d, j, t, pl.ds(col, span), :] = state[d][j]
        return carry

    lax.fori_loop(0, tiles * per, vertical, 0)

    side = lax.broadcasted_iota(jnp.int32, (cols // 2, LANES), 1) < LANES // 2
    for d in range(2):
        for j in range(2):
            vsend[d, j, 0:cols] = vtot[d, j, 0].astype(BF16)
            vsend[d, j, cols : cols + cols // 2] = jnp.where(
                side, vtot[d, j, 1, 0 : cols // 2], pltpu.roll(vtot[d, j, 1, cols // 2 : cols], LANES // 2, 1)
            ).astype(BF16)

    def totals(count, mine, name, sends, recvs, sems, semr, act, d, far):
        target = mine - far if d else mine + far
        outer = mine == count - 1 if d else mine == 0
        present = (target >= 0) & (target < count)
        for whole in (True, False):
            a, b = (sends.at[d], recvs.at[mine]) if whole else (sends.at[d, 0], recvs.at[mine, 0])

            @pl.when(present & (jnp.logical_not(outer) if whole else outer))
            def _():
                act(
                    pltpu.make_async_remote_copy(
                        a, b, sems.at[d, far], semr.at[mine], device_id={name: target}, device_id_type=MESH
                    )
                )

    def all_totals(act, *which):
        for far in range(which[0] - 1, 0, -1):
            for d in range(2):
                totals(*which, act, d, far)

    def gather(count, mine, recvs, sems, semr, total, name):
        total[...] = jnp.zeros(total.shape, F32)
        other = {name: jnp.where(mine == 0, 1, mine - 1)}
        for d in range(2):

            def one(s, carry, d=d):
                source = count - 1 - s if d else s
                ahead = source > mine if d else source < mine

                def wait(ref):
                    pltpu.make_async_remote_copy(
                        ref, ref, sems.at[d, 0], semr.at[source], device_id=other, device_id_type=MESH
                    ).wait_recv()

                @pl.when(ahead & (s == 0))
                def _():
                    wait(recvs.at[source, 0])
                    total[d] = recvs[source, 0].astype(F32)

                @pl.when(ahead & (s > 0))
                def _():
                    wait(recvs.at[source])
                    total[d] = recvs[source, 0].astype(F32) + recvs[source, 1].astype(F32) * total[d]

                return carry

            lax.fori_loop(0, count - 1, one, 0)

    vertical_set = (n_rows, r, "rows", vsend, vrecv, sem_v_s, sem_v_r)
    horizontal_set = (n_cols, c, "cols", hsend, hrecv, sem_h_s, sem_h_r)
    all_totals(lambda copy: copy.start(), *vertical_set)

    hparams = [gpar[t] for t in range(tiles)]

    def horizontal(j, states):
        new = []
        for t in range(tiles):
            for d in range(2):
                pos = cols - 1 - j if d else j
                push, kept = states[2 * t + d]
                place = pl.ds(pos, rows, stride=pitch)
                value = u[t, place, :]
                params = hparams[t]
                gate = half_mask + half_mask * jnp.tanh(params[d : d + 1] * value + params[4 + d : 5 + d])
                keep = 1.0 - gate
                push = keep * push + gate * value
                kept = keep * kept
                ph[d, t, place, :] = push
                kh[d, t, place, :] = kept
                new.append((push, kept))
        return tuple(new)

    start = tuple((jnp.zeros((rows, LANES), F32), jnp.ones((rows, LANES), F32)) for _ in range(2 * tiles))
    states = lax.fori_loop(0, cols, horizontal, start, unroll=4)
    for t in range(tiles):
        for d in range(2):
            for j in range(2):
                hsend[d, j, t] = states[2 * t + d][j].astype(BF16)
    all_totals(lambda copy: copy.start(), *horizontal_set)

    def product_z(q, carry):
        value = silu(product(q, wz)) * par[10:11, :]
        for t in range(tiles):
            zs[t, pl.ds(pl.multiple_of(q * step_rows * cols, 8), step_rows * cols), :] = value[
                :, t * LANES : (t + 1) * LANES
            ]
        return carry

    lax.fori_loop(0, rows // step_rows, product_z, 0, unroll=True)

    gather(n_cols, c, hrecv, sem_h_s, sem_h_r, ch, "cols")
    gather(n_rows, r, vrecv, sem_v_s, sem_v_r, packed, "rows")
    for d in range(2):
        last = packed[d, cols : cols + cols // 2]
        cv[d, 0] = packed[d, 0:cols]
        cv[d, 1, 0 : cols // 2] = jnp.where(side, last, 0.0)
        cv[d, 1, cols // 2 : cols] = jnp.where(side, pltpu.roll(last, LANES // 2, 1), 0.0)

    lane = lax.broadcasted_iota(jnp.int32, (cols, LANES), 1)
    halves = st.shape[0]
    per_half = rows // halves

    def stat_copy(g):
        return pltpu.make_async_remote_copy(
            st.at[g], st_other.at[g], sem_st.at[0, g], sem_st.at[1, g], device_id=at(0, 0, o), device_id_type=MESH
        )

    for g in range(halves):

        def total_row(i, stats):
            place = pl.ds(pl.multiple_of(i * cols, 8), cols)
            place_h = pl.ds(pl.multiple_of(i * pitch, 8), cols)
            one, two = 0.0, 0.0
            for t in range(tiles):
                across = (
                    ph[0, t, place_h, :] + ph[1, t, place_h, :]
                    + kh[0, t, place_h, :] * ch[0, t, pl.ds(i, 1), :]
                    + kh[1, t, place_h, :] * ch[1, t, pl.ds(i, 1), :]
                )
                along = (
                    pv[0, t, place, :] + pv[1, t, place, :]
                    + kv[0, t, place, :] * cv[0, t] + kv[1, t, place, :] * cv[1, t]
                )
                value = across + along.astype(BF16).astype(F32)
                sm[t, place, :] = value
                one = one + value
                two = two + value * value
            one = jnp.sum(one, -1, keepdims=True)
            two = jnp.sum(two, -1, keepdims=True)
            at_lane = i - g * per_half
            return jnp.where(lane == at_lane, one, jnp.where(lane == per_half + at_lane, two, stats))

        st[g] = lax.fori_loop(g * per_half, (g + 1) * per_half, total_row, jnp.zeros((cols, LANES), F32), unroll=True)
        stat_copy(g).start()

    def part_copy(q):
        place = pl.ds(q * step_rows, step_rows)
        return pltpu.make_async_remote_copy(
            psend.at[place], precv.at[place], sem_p.at[0, q], sem_p.at[1, q],
            device_id=at(0, 0, o), device_id_type=MESH,
        )

    inner = 2 * width
    chunks = rows // step_rows
    for g in range(halves):
        stat_copy(g).wait_recv()
        both = st[g] + st_other[g]

        def gate_row(i, carry):
            at_lane = i - g * per_half
            mean = jnp.sum(jnp.where(lane == at_lane, both, 0.0), -1, keepdims=True) / inner
            msq = jnp.sum(jnp.where(lane == per_half + at_lane, both, 0.0), -1, keepdims=True) / inner
            rstd = lax.rsqrt(msq - mean * mean + 1e-05)
            place = pl.ds(pl.multiple_of(i * cols, 16), cols)
            for t in range(tiles):
                gated[place, t * LANES : (t + 1) * LANES] = (
                    (sm[t, place, :] - mean) * rstd * zs[t, place, :]
                ).astype(BF16)
            return carry

        for q in range(g * chunks // halves, (g + 1) * chunks // halves):
            lax.fori_loop(q * step_rows, (q + 1) * step_rows, gate_row, 0, unroll=True)
            value = jnp.dot(
                gated[pl.ds(q * step_rows * cols, step_rows * cols), :], wo[...], preferred_element_type=F32
            ).astype(BF16)
            place = pl.ds(q * step_rows, step_rows)
            psend[place] = value[:, LANES : LANES + part].reshape(step_rows, cols, part)
            part_copy(q).start()
            pown[place] = value[:, 0:part].reshape(step_rows, cols, part)

    for q in range(chunks):
        part_copy(q).wait_recv()
        place = pl.ds(q * step_rows, step_rows)
        branch = pown[place].astype(F32) + precv[place].astype(F32)
        out[place] = (tok[place].astype(F32) + (2.0 * half_mask) * branch).astype(BF16)

    for g in range(bands):
        tok_copy(g).wait_send()
    for n, (present, *_rest) in enumerate(neighbours):

        @pl.when(present)
        def _():
            for turn, chan in enumerate((k, o)):
                halo_copy(n, turn, chan).wait_send()

    all_totals(lambda copy: copy.wait_send(), *vertical_set)
    all_totals(lambda copy: copy.wait_send(), *horizontal_set)
    for g in range(halves):
        stat_copy(g).wait_send()
    for q in range(chunks):
        part_copy(q).wait_send()


def on_device(
    n_rows, n_cols,
    tokens, tile_mask, ln_gain, w_in_x, w_in_z, conv_w, conv_b, gate_scale, gate_bias, norm_gain, w_out,
):
    rows, cols, part = tokens.shape
    width = w_in_x.shape[1]
    tiles = -(-width // LANES)
    pad = tiles * LANES
    tall = rows * cols
    pitch = cols + 8
    assert TILE % rows == 0 and TILE % cols == 0 and 2 * width == 3 * LANES
    halo_rows = 2 * cols + 2 * rows + 64
    dma = pltpu.SemaphoreType.DMA
    vmem = pl.BlockSpec(memory_space=pltpu.VMEM)
    chunks = rows // 4
    operands = (
        tokens, tile_mask, ln_gain.reshape(1, -1), w_in_x, w_in_z, conv_w, conv_b.reshape(1, -1),
        gate_scale, gate_bias, norm_gain.reshape(1, -1), w_out,
    )
    scratch = [
        (pltpu.SMEM if n == 1 else pltpu.VMEM)(x.shape, x.dtype) for n, x in enumerate(operands)
    ] + [
        dma((len(operands),)),
        pltpu.SemaphoreType.REGULAR((2, 2, max(n_rows, n_cols, 3))),

        pltpu.VMEM((rows, cols, part), BF16),
        pltpu.VMEM((rows * 32, LANES), F32),
        pltpu.VMEM((2 * rows, part), BF16),
        pltpu.VMEM((2, halo_rows, part), BF16),
        pltpu.VMEM((2, part, pad), BF16),
        pltpu.VMEM((2, part, pad), BF16),
        pltpu.VMEM((pad, 2 * LANES), BF16),
        pltpu.VMEM((16, pad), F32),
        pltpu.VMEM((tiles, 8, LANES), F32),
        pltpu.VMEM((2, rows, cols, part), BF16),
        pltpu.VMEM((halo_rows, pad), F32),
        pltpu.VMEM((tiles, rows + 2, cols + 16, LANES), F32),
        pltpu.VMEM((tiles, rows * pitch, LANES), F32),
        pltpu.VMEM((2, tiles, tall, LANES), F32),
        pltpu.VMEM((2, tiles, tall, LANES), F32),
        pltpu.VMEM((2, tiles, rows * pitch, LANES), F32),
        pltpu.VMEM((2, tiles, rows * pitch, LANES), F32),
        pltpu.VMEM((tiles, tall, LANES), F32),
        pltpu.VMEM((tiles, tall, LANES), F32),
        pltpu.VMEM((tall, pad), BF16),
        pltpu.VMEM((2, 2, tiles, cols, LANES), F32),
        pltpu.VMEM((2, cols * 3 // 2, LANES), F32),
        pltpu.VMEM((2, 2, cols * 3 // 2, LANES), BF16),
        pltpu.VMEM((n_rows, 2, cols * 3 // 2, LANES), BF16),
        pltpu.VMEM((2, 2, tiles, rows, LANES), BF16),
        pltpu.VMEM((n_cols, 2, tiles, rows, LANES), BF16),
        pltpu.VMEM((2, tiles, cols, LANES), F32),
        pltpu.VMEM((2, tiles, rows, LANES), F32),
        pltpu.VMEM((2, cols, LANES), F32),
        pltpu.VMEM((2, cols, LANES), F32),
        pltpu.VMEM((rows, cols, part), BF16),
        pltpu.VMEM((rows, cols, part), BF16),
        pltpu.VMEM((rows, cols, part), BF16),
        dma((2, 2)),
        dma((8, 2)),
        dma((8, 2)),
        dma((2, n_rows)),
        dma((n_rows,)),
        dma((2, n_cols)),
        dma((n_cols,)),
        dma((2, 2)),
        dma((2, chunks)),
    ]
    return pl.pallas_call(
        functools.partial(kernel, n_rows, n_cols, pitch),
        out_shape=pltpu.VMEM(tokens.shape, BF16),
        in_specs=[pl.BlockSpec(memory_space=pl.ANY)] * len(operands),
        out_specs=vmem,
        scratch_shapes=scratch,
        compiler_params=pltpu.CompilerParams(collective_id=0, has_side_effects=True),
    )(*operands)


def solution(mesh):
    in_specs = (
        P(("groups", "rows"), "cols", "chan"),
        P("groups", None),
        P(),
        P(None, "chan"),
        P(None, "chan"),
        P(None, None, "chan"),
        P("chan"),
        P(None, "chan"),
        P(None, "chan"),
        P("chan"),
        P("chan", None),
    )
    out_specs = P(("groups", "rows"), "cols", "chan")
    return jax.shard_map(
        functools.partial(on_device, mesh.shape["rows"], mesh.shape["cols"]),
        mesh=mesh, in_specs=in_specs, out_specs=out_specs, check_vma=False,
    )
```

profile of v0, /device:TPU:0, one launch (start us, length us, event | category | flops | bytes accessed | tf_op | source)
XLA Modules:
  0.0 20.5 jit_solution(14766527549175561616)
XLA Ops:
  0.0 19.8 %shard_map.109 = bf16[16,64,96]{2,1,0:T(8,128)(2,1)S(1)} custom-call(bf16[16,64,96]{2,1,0:T(8,128)(2,1)} %refs_0_.1, s32[1,2]{1,0:T(1,128)} %refs_1_.1, f32[1,192]{1,0:T(1,128)} %bitcast.3, bf16[192,192]{1,0:T(8,128)(2,1)} %refs_3_.1, bf16[192,192]{1,0:T(8,128)(2,1)} %refs_4_.1, f32[3,3,192]{2,1,0:T(4,128)} %refs_5_.1, f32[1,192]{1,0:T(1,128)} %bitcast.4, ...), custom_call_target="tpu_custom_call" | custom-call | tf_op jit(solution)/shard_map/pallas_call | solution.py:563
  19.8 0.7 %copy.13 = bf16[16,64,96]{2,1,0:T(8,128)(2,1)} copy(bf16[16,64,96]{2,1,0:T(8,128)(2,1)S(1)} %shard_map.109) | data formatting | bytes 393216
where the time goes:
time: 20.7 us; the launch traced here: 20.5 us
  Pallas kernels  19.8 us (96%)
  local copies, waits for them, and re-layouts  0.71 us (3%)
    pallas_call x1, Pallas kernels, on_device(): pl.pallas_call(functools.partial(kernel, n_rows, n_cols, pitch), out_shap...  19.8 us
    unnamed x1, local copies, waits for them, and re-layouts  0.71 us

commit v1 on v0

--- a/solution.py
+++ b/solution.py
@@ -43,8 +43,8 @@
     tok, tile_mask, ln_gain, w_x, w_z, conv_w, conv_b, gate_scale, gate_bias, norm_gain, w_out,
     out,
     tok_other, cells, edge, halo, wx, wz, wo, par, gpar, normed, halo_u, upad, u,
-    pv, kv, ph, kh, zs, sm, gated, vtot, packed, vsend, vrecv, hsend, hrecv, cv, ch, st, st_other, psend, precv, pown,
-    sem_tok, sem_halo_s, sem_halo_r, sem_v_s, sem_v_r, sem_h_s, sem_h_r, sem_st, sem_p,
+    pv, kv, ph, kh, zs, gated, vtot, packed, vsend, vrecv, hsend, hrecv, cv, ch, st, st_other, psend, precv, pown, bsend, brecv, bown,
+    sem_tok, sem_halo_s, sem_halo_r, sem_v_s, sem_v_r, sem_h_s, sem_h_r, sem_st, sem_p, sem_b,
 ):
     r, c, k = (lax.axis_index(name) for name in ("rows", "cols", "chan"))
     o = 1 - k
@@ -381,6 +381,7 @@
 
     def product_z(q, carry):
         value = silu(product(q, wz)) * par[10:11, :]
+        gated[pl.ds(q * step_rows * cols, step_rows * cols), :] = value.astype(BF16)
         for t in range(tiles):
             zs[t, pl.ds(pl.multiple_of(q * step_rows * cols, 8), step_rows * cols), :] = value[
                 :, t * LANES : (t + 1) * LANES
@@ -388,6 +389,26 @@
         return carry
 
     lax.fori_loop(0, rows // step_rows, product_z, 0, unroll=True)
+
+    def scale_copy(q):
+        place = pl.ds(q * step_rows, step_rows)
+        return pltpu.make_async_remote_copy(
+            bsend.at[place], brecv.at[place], sem_b.at[0, q], sem_b.at[1, q],
+            device_id=at(0, 0, o), device_id_type=MESH,
+        )
+
+    def project(q):
+        return jnp.dot(
+            gated[pl.ds(q * step_rows * cols, step_rows * cols), :], wo[...], preferred_element_type=F32
+        )
+
+    chunks = rows // step_rows
+    for q in range(chunks):
+        value = project(q)
+        place = pl.ds(q * step_rows, step_rows)
+        bsend[place] = value[:, LANES : LANES + part].astype(BF16).reshape(step_rows, cols, part)
+        scale_copy(q).start()
+        bown[place] = value[:, 0:part].reshape(step_rows, cols, part)
 
     gather(n_cols, c, hrecv, sem_h_s, sem_h_r, ch, "cols")
     gather(n_rows, r, vrecv, sem_v_s, sem_v_r, packed, "rows")
@@ -406,12 +427,21 @@
             st.at[g], st_other.at[g], sem_st.at[0, g], sem_st.at[1, g], device_id=at(0, 0, o), device_id_type=MESH
         )
 
-    for g in range(halves):
+    def part_copy(q):
+        place = pl.ds(q * step_rows, step_rows)
+        return pltpu.make_async_remote_copy(
+            psend.at[place], precv.at[place], sem_p.at[0, q], sem_p.at[1, q],
+            device_id=at(0, 0, o), device_id_type=MESH,
+        )
+
+    inner = 2 * width
+    for q in range(chunks):
+        g = q * halves // chunks
 
         def total_row(i, stats):
             place = pl.ds(pl.multiple_of(i * cols, 8), cols)
             place_h = pl.ds(pl.multiple_of(i * pitch, 8), cols)
-            one, two = 0.0, 0.0
+            one, two, values = 0.0, 0.0, []
             for t in range(tiles):
                 across = (
                     ph[0, t, place_h, :] + ph[1, t, place_h, :]
@@ -423,57 +453,47 @@
                     + kv[0, t, place, :] * cv[0, t] + kv[1, t, place, :] * cv[1, t]
                 )
                 value = across + along.astype(BF16).astype(F32)
-                sm[t, place, :] = value
+                values.append(value)
                 one = one + value
                 two = two + value * value
             one = jnp.sum(one, -1, keepdims=True)
             two = jnp.sum(two, -1, keepdims=True)
+            mean = one / width
+            for t in range(tiles):
+                gated[place, t * LANES : (t + 1) * LANES] = ((values[t] - mean) * zs[t, place, :]).astype(BF16)
             at_lane = i - g * per_half
             return jnp.where(lane == at_lane, one, jnp.where(lane == per_half + at_lane, two, stats))
 
-        st[g] = lax.fori_loop(g * per_half, (g + 1) * per_half, total_row, jnp.zeros((cols, LANES), F32), unroll=True)
-        stat_copy(g).start()
-
-    def part_copy(q):
+        stats = jnp.zeros((cols, LANES), F32) if q * halves % chunks == 0 else stats
+        stats = lax.fori_loop(q * step_rows, (q + 1) * step_rows, total_row, stats, unroll=True)
+        if (q + 1) * halves % chunks == 0:
+            st[g] = stats
+            stat_copy(g).start()
+        value = project(q)
         place = pl.ds(q * step_rows, step_rows)
-        return pltpu.make_async_remote_copy(
-            psend.at[place], precv.at[place], sem_p.at[0, q], sem_p.at[1, q],
-            device_id=at(0, 0, o), device_id_type=MESH,
-        )
-
-    inner = 2 * width
-    chunks = rows // step_rows
-    for g in range(halves):
-        stat_copy(g).wait_recv()
-        both = st[g] + st_other[g]
-
-        def gate_row(i, carry):
+        psend[place] = value[:, LANES : LANES + part].astype(BF16).reshape(step_rows, cols, part)
+        part_copy(q).start()
+        pown[place] = value[:, 0:part].reshape(step_rows, cols, part)
+
+    for q in range(chunks):
+        scale_copy(q).wait_recv()
+    for q in range(chunks):
+        g = q * halves // chunks
+        if q * halves % chunks == 0:
+            stat_copy(g).wait_recv()
+            mine, both = st[g], st[g] + st_other[g]
+            mean = both / inner
+            msq = pltpu.roll(both, LANES - per_half, 1) / inner
+            rstd = lax.rsqrt(msq - mean * mean + 1e-05)
+            shift = rstd * (mine / width - mean)
+        part_copy(q).wait_recv()
+        for i in range(q * step_rows, (q + 1) * step_rows):
             at_lane = i - g * per_half
-            mean = jnp.sum(jnp.where(lane == at_lane, both, 0.0), -1, keepdims=True) / inner
-            msq = jnp.sum(jnp.where(lane == per_half + at_lane, both, 0.0), -1, keepdims=True) / inner
-            rstd = lax.rsqrt(msq - mean * mean + 1e-05)
-            place = pl.ds(pl.multiple_of(i * cols, 16), cols)
-            for t in range(tiles):
-                gated[place, t * LANES : (t + 1) * LANES] = (
-                    (sm[t, place, :] - mean) * rstd * zs[t, place, :]
-                ).astype(BF16)
-            return carry
-
-        for q in range(g * chunks // halves, (g + 1) * chunks // halves):
-            lax.fori_loop(q * step_rows, (q + 1) * step_rows, gate_row, 0, unroll=True)
-            value = jnp.dot(
-                gated[pl.ds(q * step_rows * cols, step_rows * cols), :], wo[...], preferred_element_type=F32
-            ).astype(BF16)
-            place = pl.ds(q * step_rows, step_rows)
-            psend[place] = value[:, LANES : LANES + part].reshape(step_rows, cols, part)
-            part_copy(q).start()
-            pown[place] = value[:, 0:part].reshape(step_rows, cols, part)
-
-    for q in range(chunks):
-        part_copy(q).wait_recv()
-        place = pl.ds(q * step_rows, step_rows)
-        branch = pown[place].astype(F32) + precv[place].astype(F32)
-        out[place] = (tok[place].astype(F32) + (2.0 * half_mask) * branch).astype(BF16)
+            scale = jnp.broadcast_to(rstd[:, at_lane : at_lane + 1], (cols, part))
+            offset = jnp.broadcast_to(shift[:, at_lane : at_lane + 1], (cols, part))
+            own = (scale * pown[i] + offset * bown[i]).astype(BF16).astype(F32)
+            other = (scale * precv[i].astype(F32) - offset * brecv[i].astype(F32)).astype(BF16).astype(F32)
+            out[i] = (tok[i].astype(F32) + (2.0 * half_mask) * (own + other)).astype(BF16)
 
     for g in range(bands):
         tok_copy(g).wait_send()
@@ -490,6 +510,7 @@
         stat_copy(g).wait_send()
     for q in range(chunks):
         part_copy(q).wait_send()
+        scale_copy(q).wait_send()
 
 
 def on_device(
@@ -535,7 +556,6 @@
         pltpu.VMEM((2, tiles, rows * pitch, LANES), F32),
         pltpu.VMEM((2, tiles, rows * pitch, LANES), F32),
         pltpu.VMEM((tiles, tall, LANES), F32),
-        pltpu.VMEM((tiles, tall, LANES), F32),
         pltpu.VMEM((tall, pad), BF16),
         pltpu.VMEM((2, 2, tiles, cols, LANES), F32),
         pltpu.VMEM((2, cols * 3 // 2, LANES), F32),
@@ -549,7 +569,10 @@
         pltpu.VMEM((2, cols, LANES), F32),
         pltpu.VMEM((rows, cols, part), BF16),
         pltpu.VMEM((rows, cols, part), BF16),
+        pltpu.VMEM((rows, cols, part), F32),
         pltpu.VMEM((rows, cols, part), BF16),
+        pltpu.VMEM((rows, cols, part), BF16),
+        pltpu.VMEM((rows, cols, part), F32),
         dma((2, 2)),
         dma((8, 2)),
         dma((8, 2)),
@@ -558,6 +581,7 @@
         dma((2, n_cols)),
         dma((n_cols,)),
         dma((2, 2)),
+        dma((2, chunks)),
         dma((2, chunks)),
     ]
     return pl.pallas_call(

time: 20.7 us -> 19.9 us (0.961)
  the two profiles are of different devices: /device:TPU:0 before, /device:TPU:1 now
where the time goes in v1:
time: 19.9 us; the launch traced here: 19.7 us
  Pallas kernels  19 us (95%)
  local copies, waits for them, and re-layouts  0.71 us (4%)
    pallas_call x1, Pallas kernels, on_device(): pl.pallas_call(functools.partial(kernel, n_rows, n_cols, pitch), out_shap...  19 us
    unnamed x1, local copies, waits for them, and re-layouts  0.71 us

profile of v1, /device:TPU:1, one launch (start us, length us, event | category | flops | bytes accessed | tf_op | source)
XLA Modules:
  0.0 19.7 jit_solution(11093246245749758875)
XLA Ops:
  0.0 19.0 %shard_map.109 = bf16[16,64,96]{2,1,0:T(8,128)(2,1)S(1)} custom-call(bf16[16,64,96]{2,1,0:T(8,128)(2,1)} %refs_0_.1, s32[1,2]{1,0:T(1,128)} %refs_1_.1, f32[1,192]{1,0:T(1,128)} %bitcast.3, bf16[192,192]{1,0:T(8,128)(2,1)} %refs_3_.1, bf16[192,192]{1,0:T(8,128)(2,1)} %refs_4_.1, f32[3,3,192]{2,1,0:T(4,128)} %refs_5_.1, f32[1,192]{1,0:T(1,128)} %bitcast.4, ...), custom_call_target="tpu_custom_call" | custom-call | tf_op jit(solution)/shard_map/pallas_call | solution.py:587
  19.0 0.7 %copy.13 = bf16[16,64,96]{2,1,0:T(8,128)(2,1)} copy(bf16[16,64,96]{2,1,0:T(8,128)(2,1)S(1)} %shard_map.109) | data formatting | bytes 393216
